TPU v7x, 32 devices: a whole 2x2x4 slice. The times are simulated.
32 devices in a mesh: section: 2 (over y), rows: 4 (over z), heads: 4 (over x, core).
Axes of the slice: x: 2, y: 2, z: 4, core: 2. Of those that a mesh axis runs over, the one named last changes fastest.
Arguments:
- tokens: bfloat16 [2, 2048, 4, 1024], P('section', 'heads', 'rows'), may hold values from -6 to 6
- image_lengths: int32 [2, 4, 6], P(None, 'rows'), may hold values from 64 to 576, as said below
- tile_ranks: int32 [2, 4, 6], P(None, 'rows'), may hold values from 0 to 5, each once within a row
- w_qkv: bfloat16 [1024, 3, 1024], P(None, None, 'heads'), may hold values from -0.1875 to 0.1875
- bias_qv: bfloat16 [2, 1024], P(None, 'heads'), may hold values from -3 to 3
- w_out: bfloat16 [1024, 1024], P('heads'), may hold values from -1.5 to 1.5
- bias_out: bfloat16 [1024], replicated, may hold values from -3 to 3
- w_up: bfloat16 [1024, 4096], P(None, 'heads'), may hold values from -0.1875 to 0.1875
- bias_up: bfloat16 [4096], P('heads'), may hold values from -3 to 3
- w_down: bfloat16 [4096, 1024], P('heads'), may hold values from -0.09375 to 0.09375
- bias_down: bfloat16 [1024], replicated, may hold values from -3 to 3
- ln1_gain: bfloat16 [1024], replicated, may hold values from 0.5 to 1.5
- ln1_bias: bfloat16 [1024], replicated, may hold values from -3 to 3
- ln2_gain: bfloat16 [1024], replicated, may hold values from 0.5 to 1.5
- ln2_bias: bfloat16 [1024], replicated, may hold values from -3 to 3
- grad_out: bfloat16 [2, 2048, 4, 1024], P(None, None, 'rows', ('section', 'heads')), may hold values from -6 to 6
- grad_tap: bfloat16 [2, 2048, 4, 1024], P(None, None, 'rows', ('section', 'heads')), may hold values from -6 to 6
Outputs:
- block_output: bfloat16 [2, 2048, 4, 1024], P(None, None, 'rows', ('section', 'heads'))
- input_tap: bfloat16 [2, 2048, 4, 1024], P(None, None, 'rows', ('section', 'heads'))
- grad_tokens: float32 [2, 2048, 4, 1024], P('section', 'heads', 'rows')
- grad_w_qkv: float32 [1024, 3, 1024], P(None, None, 'heads')
- grad_bias_qv: float32 [2, 1024], P(None, 'heads')
- grad_w_out: float32 [1024, 1024], P('heads')
- grad_bias_out: float32 [1024], replicated
- grad_w_up: float32 [1024, 4096], P(None, 'heads')
- grad_bias_up: float32 [4096], P('heads')
- grad_w_down: float32 [4096, 1024], P('heads')
- grad_bias_down: float32 [1024], replicated
- grad_ln1_gain: float32 [1024], replicated
- grad_ln1_bias: float32 [1024], replicated
- grad_ln2_gain: float32 [1024], replicated
- grad_ln2_bias: float32 [1024], replicated
Inputs may be any that keep to these rules, and one draw needn't show every extreme that they name: `image_lengths`: each row holds the patch counts of the 6 images of one sequence, in packing order, summing to 1920; the remaining positions of the 2048 are padding; every row has an image of exactly 576 patches and one of exactly 64. `tile_ranks`: each row is an ordering of the images 0 to 5: their places in the decoder's order.
All inputs are finite; a program needn't handle non-finite values.
Results may differ from a plain program's by a relative error of at most 0.024.
Values may be sent and summed in bfloat16 or wider, within the bound.
A program may use at most 192 MiB of HBM per device.

v0:
```python
from functools import partial
import jax
import jax.numpy as jnp
from jax import lax
from jax.sharding import PartitionSpec as P

HD = 64
EPSILON = 1e-06
MASKED = -1e30


def layer_norm(values_in, norm_gain, norm_shift):
    average = jnp.mean(values_in, axis=-1, keepdims=True)
    centred = values_in - average
    variance = jnp.mean(centred * centred, axis=-1, keepdims=True)
    return centred * lax.rsqrt(variance + EPSILON) * norm_gain + norm_shift


def gelu_exact(values_in):
    return jax.nn.gelu(values_in, approximate=False)


def image_tables(lengths, tile_order, extent):
    image_ends = jnp.cumsum(lengths)
    image_starts = image_ends - lengths
    earlier = (tile_order[None, :] < tile_order[:, None]).astype(jnp.int32)
    new_starts = jnp.sum(earlier * lengths[None, :], axis=1)
    position = jnp.arange(extent, dtype=jnp.int32)
    segment = jnp.sum((position[:, None] >= image_ends[None, :]).astype(jnp.int32), axis=1)
    inside_new = (position[:, None] >= new_starts[None, :]) & (
        position[:, None] < (new_starts + lengths)[None, :]
    )
    source = position + jnp.sum(jnp.where(inside_new, image_starts - new_starts, 0), axis=1)
    inside_old = segment[:, None] == jnp.arange(lengths.shape[0], dtype=jnp.int32)[None, :]
    target = position + jnp.sum(jnp.where(inside_old, new_starts - image_starts, 0), axis=1)
    return (segment, source, target)


def reorder_pair(first_rows, second_rows, picks):
    extent = picks.shape[-1]
    columns = jnp.arange(extent, dtype=jnp.int32)
    selector = (picks[..., None] == columns).astype(jnp.bfloat16)
    first_out = jnp.einsum(
        "hspq,hqsc->hpsc", selector, first_rows, preferred_element_type=jnp.float32
    )
    second_out = jnp.einsum(
        "hspq,hqsc->hpsc", selector, second_rows, preferred_element_type=jnp.float32
    )
    return (first_out.astype(jnp.bfloat16), second_out.astype(jnp.bfloat16))


def masked_scores(queries, key_seq, segment_rows, segment_seq):
    scores = jnp.einsum(
        "qhd,khd->hqk", queries, key_seq, preferred_element_type=jnp.float32
    ) * HD ** (-0.5)
    allowed = segment_rows[:, None] == segment_seq[None, :]
    return jnp.where(allowed[None], scores, MASKED)


def attend_forward(query_seq, key_seq, value_seq, segment_seq, block_rows):
    extent = query_seq.shape[0]
    block_count = extent // block_rows
    query_blocks = query_seq.reshape((block_count, block_rows) + query_seq.shape[1:])
    segment_blocks = segment_seq.reshape(block_count, block_rows)

    def one_block(block_item):
        queries, segment_rows = block_item
        scores = masked_scores(queries, key_seq, segment_rows, segment_seq)
        row_max = jnp.max(scores, axis=-1, keepdims=True)
        exponent = jnp.exp(scores - row_max)
        row_total = jnp.sum(exponent, axis=-1, keepdims=True)
        attend_prob = (exponent / row_total).astype(jnp.bfloat16)
        mixture = jnp.einsum(
            "hqk,khd->qhd", attend_prob, value_seq, preferred_element_type=jnp.float32
        )
        return (mixture, (row_max + jnp.log(row_total))[..., 0])

    mixture, log_sum = lax.map(one_block, (query_blocks, segment_blocks))
    return (mixture.reshape(query_seq.shape), log_sum)


def attend_backward(query_seq, key_seq, value_seq, segment_seq, log_sum, grad_seq, block_rows):
    extent = query_seq.shape[0]
    block_count = extent // block_rows
    query_blocks = query_seq.reshape((block_count, block_rows) + query_seq.shape[1:])
    grad_blocks = grad_seq.reshape((block_count, block_rows) + grad_seq.shape[1:])
    segment_blocks = segment_seq.reshape(block_count, block_rows)

    def one_block(running, block_item):
        key_acc, value_acc = running
        queries, segment_rows, log_rows, grad_rows = block_item
        scores = masked_scores(queries, key_seq, segment_rows, segment_seq)
        attend_prob = jnp.exp(scores - log_rows[..., None])
        prob_low = attend_prob.astype(jnp.bfloat16)
        grad_prob = jnp.einsum(
            "qhd,khd->hqk", grad_rows, value_seq, preferred_element_type=jnp.float32
        )
        inner = jnp.sum(attend_prob * grad_prob, axis=-1, keepdims=True)
        grad_score = (attend_prob * (grad_prob - inner) * HD ** (-0.5)).astype(jnp.bfloat16)
        grad_query = jnp.einsum(
            "hqk,khd->qhd", grad_score, key_seq, preferred_element_type=jnp.float32
        )
        key_acc = key_acc + jnp.einsum(
            "hqk,qhd->khd", grad_score, queries, preferred_element_type=jnp.float32
        )
        value_acc = value_acc + jnp.einsum(
            "hqk,qhd->khd", prob_low, grad_rows, preferred_element_type=jnp.float32
        )
        return ((key_acc, value_acc), grad_query)

    zero_rows = jnp.zeros(key_seq.shape, jnp.float32)
    (grad_key, grad_value), grad_query = lax.scan(
        one_block, (zero_rows, zero_rows), (query_blocks, segment_blocks, log_sum, grad_blocks)
    )
    return (grad_query.reshape(query_seq.shape), grad_key, grad_value)


def per_device(
    tokens,
    image_lengths,
    tile_ranks,
    w_qkv,
    bias_qv,
    w_out,
    bias_out,
    w_up,
    bias_up,
    w_down,
    bias_down,
    ln1_gain,
    ln1_bias,
    ln2_gain,
    ln2_bias,
    grad_out,
    grad_tap,
):
    own_tokens = tokens[0]
    part_rows = own_tokens.shape[0]
    seq_count = own_tokens.shape[1]
    full_len = part_rows * lax.axis_size("heads")
    block_rows = min(512, full_len)
    section_at = lax.axis_index("section")
    head_at = lax.axis_index("heads")
    halves = image_lengths.shape[0]
    image_count = image_lengths.shape[2]
    flat_lengths = image_lengths.reshape(halves * seq_count, image_count)
    flat_orders = tile_ranks.reshape(halves * seq_count, image_count)
    segments, sources, targets = jax.vmap(partial(image_tables, extent=full_len))(
        flat_lengths, flat_orders
    )
    segments = segments.reshape(halves, seq_count, full_len)
    sources = sources.reshape(halves, seq_count, full_len)
    targets = targets.reshape(halves, seq_count, full_len)
    own_segments = lax.dynamic_index_in_dim(segments, section_at, 0, keepdims=False)
    row_places = head_at * part_rows + jnp.arange(part_rows, dtype=jnp.int32)
    valid_rows = (
        (jnp.take(own_segments, row_places, axis=1) < image_count).astype(jnp.float32).T[:, :, None]
    )
    token_values = own_tokens.astype(jnp.float32)
    normed_one = layer_norm(token_values, ln1_gain, ln1_bias).astype(jnp.bfloat16)
    gathered_one = lax.all_gather(normed_one, "heads", axis=0, tiled=True)
    projected = jnp.einsum("rsd,dck->rsck", gathered_one, w_qkv, preferred_element_type=jnp.float32)
    query_all = (projected[:, :, 0] + bias_qv[0]).astype(jnp.bfloat16)
    key_all = projected[:, :, 1].astype(jnp.bfloat16)
    value_all = (projected[:, :, 2] + bias_qv[1]).astype(jnp.bfloat16)
    head_groups = query_all.shape[2] // HD
    split_shape = (full_len, seq_count, head_groups, HD)
    query_heads = query_all.reshape(split_shape)
    key_heads = key_all.reshape(split_shape)
    value_heads = value_all.reshape(split_shape)
    which = 0
    mixture, log_sum = attend_forward(
        query_heads[:, which],
        key_heads[:, which],
        value_heads[:, which],
        own_segments[which],
        block_rows,
    )
    mixtures = [mixture]
    log_sums = [log_sum]
    attended = (
        jnp.stack(mixtures, axis=1)
        .reshape(full_len, seq_count, head_groups * HD)
        .astype(jnp.bfloat16)
    )
    picked = attended
    attn_sum = (
        lax.psum_scatter(
            jnp.einsum("rsk,kd->rsd", picked, w_out, preferred_element_type=jnp.float32).astype(
                jnp.bfloat16
            ),
            "heads",
            scatter_dimension=0,
            tiled=True,
        ).astype(jnp.float32)
        + bias_out
    )
    after_attn = token_values + attn_sum
    normed_two = layer_norm(after_attn, ln2_gain, ln2_bias).astype(jnp.bfloat16)
    gathered_two = lax.all_gather(normed_two, "heads", axis=0, tiled=True)
    pre_act = (
        jnp.einsum("rsd,df->rsf", gathered_two, w_up, preferred_element_type=jnp.float32) + bias_up
    )
    activated = gelu_exact(pre_act).astype(jnp.bfloat16)
    picked = activated
    mlp_sum = (
        lax.psum_scatter(
            jnp.einsum("rsf,fd->rsd", picked, w_down, preferred_element_type=jnp.float32).astype(
                jnp.bfloat16
            ),
            "heads",
            scatter_dimension=0,
            tiled=True,
        ).astype(jnp.float32)
        + bias_down
    )
    block_out = ((after_attn + mlp_sum) * valid_rows).astype(jnp.bfloat16)
    sent_out, sent_tap = (
        lax.all_to_all(block_out, ("section", "heads"), split_axis=2, concat_axis=0, tiled=True),
        lax.all_to_all(own_tokens, ("section", "heads"), split_axis=2, concat_axis=0, tiled=True),
    )
    decoder_shape = (halves, full_len, seq_count, sent_out.shape[2])
    output_dec, tap_dec = reorder_pair(
        sent_out.reshape(decoder_shape), sent_tap.reshape(decoder_shape), sources
    )
    encoder_shape = (halves * full_len, seq_count, grad_out.shape[3])
    back_out, back_tap = reorder_pair(grad_out, grad_tap, targets)
    grad_block, grad_direct = (
        lax.all_to_all(
            back_out.reshape(encoder_shape),
            ("section", "heads"),
            split_axis=0,
            concat_axis=2,
            tiled=True,
        ),
        lax.all_to_all(
            back_tap.reshape(encoder_shape),
            ("section", "heads"),
            split_axis=0,
            concat_axis=2,
            tiled=True,
        ),
    )
    grad_mlp_full = grad_block.astype(jnp.float32) * valid_rows
    grad_mlp = grad_mlp_full.astype(jnp.bfloat16)
    grad_b_down = jnp.sum(grad_mlp, axis=(0, 1), dtype=jnp.float32)
    grad_mlp_all = lax.all_gather(grad_mlp, "heads", axis=0, tiled=True)
    grad_w_down_part = jnp.einsum(
        "rsf,rsd->fd", activated, grad_mlp_all, preferred_element_type=jnp.float32
    )
    grad_act = jnp.einsum("rsd,fd->rsf", grad_mlp_all, w_down, preferred_element_type=jnp.float32)
    gelu_back = jax.vjp(gelu_exact, pre_act)[1]
    grad_pre = gelu_back(grad_act)[0].astype(jnp.bfloat16)
    grad_w_up_part = jnp.einsum(
        "rsd,rsf->df", gathered_two, grad_pre, preferred_element_type=jnp.float32
    )
    grad_b_up = jnp.sum(grad_pre, axis=(0, 1), dtype=jnp.float32)
    picked = grad_pre
    grad_normed_two = lax.psum_scatter(
        jnp.einsum("rsf,df->rsd", picked, w_up, preferred_element_type=jnp.float32).astype(
            jnp.bfloat16
        ),
        "heads",
        scatter_dimension=0,
        tiled=True,
    ).astype(jnp.float32)
    norm_two_back = jax.vjp(layer_norm, after_attn, ln2_gain, ln2_bias)[1]
    grad_after, grad_gain_two, grad_shift_two = norm_two_back(grad_normed_two)
    grad_after = grad_after + grad_mlp_full
    grad_attn = grad_after.astype(jnp.bfloat16)
    grad_b_out = jnp.sum(grad_attn, axis=(0, 1), dtype=jnp.float32)
    grad_attn_all = lax.all_gather(grad_attn, "heads", axis=0, tiled=True)
    grad_w_out_part = jnp.einsum(
        "rsk,rsd->kd", attended, grad_attn_all, preferred_element_type=jnp.float32
    )
    grad_attended = (
        jnp.einsum("rsd,kd->rsk", grad_attn_all, w_out, preferred_element_type=jnp.float32)
        .astype(jnp.bfloat16)
        .reshape(split_shape)
    )
    which = 0
    grad_query, grad_key, grad_value = attend_backward(
        query_heads[:, which],
        key_heads[:, which],
        value_heads[:, which],
        own_segments[which],
        log_sums[which],
        grad_attended[:, which],
        block_rows,
    )
    query_grads = [grad_query]
    key_grads = [grad_key]
    value_grads = [grad_value]
    flat_shape = (full_len, seq_count, head_groups * HD)
    grad_query_all = jnp.stack(query_grads, axis=1).reshape(flat_shape).astype(jnp.bfloat16)
    grad_key_all = jnp.stack(key_grads, axis=1).reshape(flat_shape).astype(jnp.bfloat16)
    grad_value_all = jnp.stack(value_grads, axis=1).reshape(flat_shape).astype(jnp.bfloat16)
    grad_projected = jnp.stack([grad_query_all, grad_key_all, grad_value_all], axis=2)
    grad_w_qkv_part = jnp.einsum(
        "rsd,rsck->dck", gathered_one, grad_projected, preferred_element_type=jnp.float32
    )
    grad_b_qv = jnp.stack(
        [
            jnp.sum(grad_query_all, axis=(0, 1), dtype=jnp.float32),
            jnp.sum(grad_value_all, axis=(0, 1), dtype=jnp.float32),
        ]
    )
    picked = grad_projected
    grad_normed_one = lax.psum_scatter(
        jnp.einsum("rsck,dck->rsd", picked, w_qkv, preferred_element_type=jnp.float32).astype(
            jnp.bfloat16
        ),
        "heads",
        scatter_dimension=0,
        tiled=True,
    ).astype(jnp.float32)
    norm_one_back = jax.vjp(layer_norm, token_values, ln1_gain, ln1_bias)[1]
    grad_input, grad_gain_one, grad_shift_one = norm_one_back(grad_normed_one)
    grad_tokens = grad_input + grad_after + grad_direct.astype(jnp.float32)
    (
        grad_w_qkv_part,
        grad_b_qv,
        grad_w_out_part,
        grad_b_out,
        grad_gain_one,
        grad_shift_one,
        grad_w_up_part,
        grad_b_up,
        grad_w_down_part,
        grad_b_down,
        grad_gain_two,
        grad_shift_two,
    ) = (
        lax.psum(grad_w_qkv_part.astype(jnp.bfloat16), ("section", "rows")).astype(jnp.float32),
        lax.psum(grad_b_qv.astype(jnp.bfloat16), ("section", "rows")).astype(jnp.float32),
        lax.psum(grad_w_out_part.astype(jnp.bfloat16), ("section", "rows")).astype(jnp.float32),
        lax.psum(grad_b_out.astype(jnp.bfloat16), ("section", "rows")).astype(jnp.float32),
        lax.psum(grad_gain_one, ("section", "rows")).astype(jnp.float32),
        lax.psum(grad_shift_one, ("section", "rows")).astype(jnp.float32),
        lax.psum(grad_w_up_part.astype(jnp.bfloat16), ("section", "rows")).astype(jnp.float32),
        lax.psum(grad_b_up.astype(jnp.bfloat16), ("section", "rows")).astype(jnp.float32),
        lax.psum(grad_w_down_part.astype(jnp.bfloat16), ("section", "rows")).astype(jnp.float32),
        lax.psum(grad_b_down.astype(jnp.bfloat16), ("section", "rows")).astype(jnp.float32),
        lax.psum(grad_gain_two, ("section", "rows")).astype(jnp.float32),
        lax.psum(grad_shift_two, ("section", "rows")).astype(jnp.float32),
    )
    grad_b_out, grad_b_down, grad_gain_one, grad_shift_one, grad_gain_two, grad_shift_two = (
        lax.psum(
            (grad_b_out, grad_b_down, grad_gain_one, grad_shift_one, grad_gain_two, grad_shift_two),
            "heads",
        )
    )
    return (
        output_dec,
        tap_dec,
        grad_tokens[None],
        grad_w_qkv_part,
        grad_b_qv,
        grad_w_out_part,
        grad_b_out,
        grad_w_up_part,
        grad_b_up,
        grad_w_down_part,
        grad_b_down,
        grad_gain_one,
        grad_shift_one,
        grad_gain_two,
        grad_shift_two,
    )


def solution(mesh):
    placed = (
        P("section", "heads", "rows", None),
        P(None, "rows", None),
        P(None, "rows", None),
        P(None, None, "heads"),
        P(None, "heads"),
        P("heads", None),
        P(),
        P(None, "heads"),
        P("heads"),
        P("heads", None),
        P(),
        P(),
        P(),
        P(),
        P(),
        P(None, None, "rows", ("section", "heads")),
        P(None, None, "rows", ("section", "heads")),
    )
    return jax.shard_map(
        per_device,
        mesh=mesh,
        in_specs=placed,
        out_specs=(
            P(None, None, "rows", ("section", "heads")),
            P(None, None, "rows", ("section", "heads")),
            P("section", "heads", "rows", None),
            P(None, None, "heads"),
            P(None, "heads"),
            P("heads", None),
            P(),
            P(None, "heads"),
            P("heads"),
            P("heads", None),
            P(),
            P(),
            P(),
            P(),
            P(),
        ),
        check_vma=False,
    )
```

profile of v0, /device:TPU:0, one launch (start us, length us, event | category | flops | bytes accessed | tf_op | source)
XLA Modules:
  0.0 1077.3 jit_solution(13621030071722300098)
XLA Ops:
  17.5 35.0 %all-gather.5.cloned.1.call-done = bf16[2048,1,1024]{2,0,1:T(8,128)(2,1)} async-done(((bf16[512,1,1024]{2,0,1:T(8,128)(2,1)}), bf16[2048,1,1024]{2,0,1:T(8,128)(2,1)}) %all-gather.5.cloned.1.call-update) | async-done | bytes 4194320 | tf_op jit(solution)/shard_map/all_gather | solution.py:161
  52.5 5.8 fusion.115
  69.9 62.9 %while.27 = (s32[]{:T(128)}, bf16[4,512,4,64]{1,3,2,0:T(8,128)(2,1)}, f32[4,4,512]{2,1,0:T(4,128)}, s32[4,512]{1,0:T(4,128)S(1)}, s32[1,2048]{1,0:T(1,128)S(1)},...) while((s32[]{:T(128)}, ...), condition=%wide.region_7.8_spmd, body=%wide.region_4.7_spmd.sunk | while | flops 1125120000 | bytes 70072528 | solution.py:78
  70.6 4.5 fusion.230
  75.1 4.4 fusion.231
  79.6 5.1 fusion.232
  86.3 4.5 fusion.230
  90.8 4.4 fusion.231
  95.3 5.1 fusion.232
  102.0 4.5 fusion.230
  106.5 4.4 fusion.231
  111.0 5.1 fusion.232
  117.7 4.5 fusion.230
  122.2 4.4 fusion.231
  126.6 5.1 fusion.232
  139.7 44.5 %reduce-scatter.5.cloned.1.call-done = bf16[512,1,1024]{2,0,1:T(8,128)(2,1)} async-done(((bf16[2048,1,1024]{2,0,1:T(8,128)(2,1)}), bf16[512,1,1024]{2,0,1:T(8,128)(2,1)}) %reduce-scatter.5.cloned.1.call-update) | async-done | bytes 1048592 | tf_op jit(solution)/shard_map/reduce_scatter | solution.py:188
  191.5 7.9 fusion.130
  212.9 22.5 %all-to-all-done.2 = bf16[8,2,32768]{2,1,0:T(2,128)(2,1)} async-done(((bf16[8,2,32768]{2,1,0:T(2,128)(2,1)}), bf16[8,2,32768]{2,1,0:T(2,128)(2,1)}, u32[]{:S(2)}, u32[]{:S(2)}) %all-to-all-start.2) | async-done | bytes 1048608 | tf_op jit(solution)/shard_map/all_to_all | solution.py:229
  235.3 5.8 reshape.983
  245.8 25.9 %multiply_convert_fusion.1 = (bf16[2048,1024]{1,0:T(8,128)(2,1)}, f32[2048,1024]{1,0:T(8,128)}, f32[2048,1024]{1,0:T(8,128)}) fusion(f32[1024]{0:T(1024)S(1)} %convert_element_type.441, bf16[1024,1024]{1,0:T(8,128)(2,1)S(1)} %copy-done, bf16[2048,1,1024]{2,0,1:T(8,128)(2,1)} %all-gather.7.cloned.1.call-done), kind=kOutput, calls=%fused_computation.81 | convolution fusion | flops 4433379328 | bytes 27267072 | tf_op jit(solution)/shard_map/rsd,df->rsf/dot_general | solution.py:202
  271.7 7.7 all-gather.9.cloned.1.call-done
  279.4 13.9 %fusion.186 = (bf16[1024]{0:T(1024)(128)(2,1)}, bf16[2048,1024]{1,0:T(8,128)(2,1)S(1)}) fusion(f32[2048,1024]{1,0:T(8,128)} %get-tuple-element.358, bf16[1024,1024]{1,0:T(8,128)(2,1)} %param.30, bf16[2048,1,1024]{2,0,1:T(8,128)(2,1)} %all-gather.9.cloned.1.call-done, f32[2048,1024]{1,0:T(8,128)} %get-tuple-element.369, f32[1024]{0:T(1024)S(1)} %convert_element_type.441), kind=kOutput, calls=%fused_computation.215 | convolution fusion | flops 4328520704 | bytes 27269120 | tf_op jit(solution)/shard_map/rsd,fd->rsf/dot_general | solution.py:251
  295.3 6.1 convert_bitcast_fusion
  303.0 8.8 convert_bitcast_fusion.1
  312.4 33.6 %reduce-scatter.9.cloned.1.call-done = bf16[512,1,1024]{2,0,1:T(8,128)(2,1)} async-done(((bf16[2048,1,1024]{2,0,1:T(8,128)(2,1)}), bf16[512,1,1024]{2,0,1:T(8,128)(2,1)}) %reduce-scatter.9.cloned.1.call-update) | async-done | bytes 1048592 | tf_op jit(solution)/shard_map/reduce_scatter | solution.py:259
  348.0 45.0 %reduce-scatter.7.cloned.1.call-done = bf16[512,1,1024]{2,0,1:T(8,128)(2,1)} async-done(((bf16[2048,1,1024]{2,0,1:T(8,128)(2,1)}), bf16[512,1,1024]{2,0,1:T(8,128)(2,1)}) %reduce-scatter.7.cloned.1.call-update) | async-done | bytes 1048592 | tf_op jit(solution)/shard_map/reduce_scatter | solution.py:207
  393.0 4.6 fusion.141
  400.9 9.5 fusion.150
  410.4 5.8 fusion.147
  416.2 19.3 %all-gather.11.cloned.1.call-done = bf16[2048,1,1024]{2,0,1:T(8,128)(2,1)} async-done(((bf16[512,1,1024]{2,0,1:T(8,128)(2,1)}), bf16[2048,1,1024]{2,0,1:T(8,128)(2,1)}) %all-gather.11.cloned.1.call-update) | async-done | bytes 4194320 | tf_op jit(solution)/shard_map/all_gather | solution.py:272
  445.9 282.8 %while.28 = (s32[]{:T(128)}, f32[2048,4,64]{0,2,1:T(8,128)}, f32[2048,4,64]{0,2,1:T(8,128)}, bf16[4,512,4,64]{1,3,2,0:T(8,128)(2,1)}, bf16[4,512,4,64]{1,3,2,0:T...) while((s32[]{:T(128)}, f32[2048,4,64]{0,2,1:T(8,128)}, ...), condition=%wide.region_20.21_spmd.clone, body=%wide.region_18.20_spmd.clone.sunk | while | flops 2796560384 | bytes 275323104 | solution.py:112
  450.9 6.8 fusion.246
  457.7 8.1 fusion.243
  465.8 24.0 %fusion.247 = bf16[4,512,4,64]{1,3,2,0:T(8,128)(2,1)} fusion(bf16[4,512,4,64]{1,3,2,0:T(8,128)(2,1)} %get-tuple-element.537, s32[]{:T(128)S(6)} %copy.184, bf16[2048,4,64]{0,2,1:T(8,128)(2,1)S(1)} %get-tuple-element.554, f32[4,512,2048]{2,1,0:T(8,128)} %fusion.243, f32[4,512,2048]{2,1,0:T(8,128)} %copy-done.2, ...), kind=kOutput, calls=%fused_computation.42.clone.1 | convolution fusion | flops 583012352 | bytes 70795264 | tf_op jit(solution)/shard_map/while/body/eval_jaxpr/hqk,khd->qhd/dot_general | solution.py:100
  489.8 25.5 %fusion.245 = f32[2048,4,64]{0,2,1:T(8,128)} fusion(f32[4,512,2048]{2,1,0:T(8,128)} %fusion.243, f32[4,512,2048]{2,1,0:T(8,128)} %copy-done.2, f32[4,512]{1,0:T(4,128)S(1)} %dynamic-slice_bitcast_fusion.2, pred[512,2048]{1,0:T(8,128)(4,1)S(1)} %broadcast_compare_fusion.5, f32[2048,4,64]{0,2,1:T(8,128)} %get-tuple-element.535, pred[]{:T(512)S(6)} %compare.3, ...), kind=kOutput, calls=%fused_computation.39.clone.1 | convolution fusion | flops 584060928 | bytes 73678856 | tf_op jit(solution)/shard_map/while/body/eval_jaxpr/hqk,qhd->khd/dot_general | solution.py:103
  520.1 8.0 fusion.246
  528.1 8.1 fusion.243
  536.2 24.0 %fusion.247 = bf16[4,512,4,64]{1,3,2,0:T(8,128)(2,1)} fusion(bf16[4,512,4,64]{1,3,2,0:T(8,128)(2,1)} %get-tuple-element.537, s32[]{:T(128)S(6)} %copy.184, bf16[2048,4,64]{0,2,1:T(8,128)(2,1)S(1)} %get-tuple-element.554, f32[4,512,2048]{2,1,0:T(8,128)} %fusion.243, f32[4,512,2048]{2,1,0:T(8,128)} %copy-done.2, ...), kind=kOutput, calls=%fused_computation.42.clone.1 | convolution fusion | flops 583012352 | bytes 70795264 | tf_op jit(solution)/shard_map/while/body/eval_jaxpr/hqk,khd->qhd/dot_general | solution.py:100
  560.2 26.1 %fusion.245 = f32[2048,4,64]{0,2,1:T(8,128)} fusion(f32[4,512,2048]{2,1,0:T(8,128)} %fusion.243, f32[4,512,2048]{2,1,0:T(8,128)} %copy-done.2, f32[4,512]{1,0:T(4,128)S(1)} %dynamic-slice_bitcast_fusion.2, pred[512,2048]{1,0:T(8,128)(4,1)S(1)} %broadcast_compare_fusion.5, f32[2048,4,64]{0,2,1:T(8,128)} %get-tuple-element.535, pred[]{:T(512)S(6)} %compare.3, ...), kind=kOutput, calls=%fused_computation.39.clone.1 | convolution fusion | flops 584060928 | bytes 73678856 | tf_op jit(solution)/shard_map/while/body/eval_jaxpr/hqk,qhd->khd/dot_general | solution.py:103
  591.1 8.0 fusion.246
  599.1 8.1 fusion.243
  607.2 24.0 %fusion.247 = bf16[4,512,4,64]{1,3,2,0:T(8,128)(2,1)} fusion(bf16[4,512,4,64]{1,3,2,0:T(8,128)(2,1)} %get-tuple-element.537, s32[]{:T(128)S(6)} %copy.184, bf16[2048,4,64]{0,2,1:T(8,128)(2,1)S(1)} %get-tuple-element.554, f32[4,512,2048]{2,1,0:T(8,128)} %fusion.243, f32[4,512,2048]{2,1,0:T(8,128)} %copy-done.2, ...), kind=kOutput, calls=%fused_computation.42.clone.1 | convolution fusion | flops 583012352 | bytes 70795264 | tf_op jit(solution)/shard_map/while/body/eval_jaxpr/hqk,khd->qhd/dot_general | solution.py:100
  631.2 26.1 %fusion.245 = f32[2048,4,64]{0,2,1:T(8,128)} fusion(f32[4,512,2048]{2,1,0:T(8,128)} %fusion.243, f32[4,512,2048]{2,1,0:T(8,128)} %copy-done.2, f32[4,512]{1,0:T(4,128)S(1)} %dynamic-slice_bitcast_fusion.2, pred[512,2048]{1,0:T(8,128)(4,1)S(1)} %broadcast_compare_fusion.5, f32[2048,4,64]{0,2,1:T(8,128)} %get-tuple-element.535, pred[]{:T(512)S(6)} %compare.3, ...), kind=kOutput, calls=%fused_computation.39.clone.1 | convolution fusion | flops 584060928 | bytes 73678856 | tf_op jit(solution)/shard_map/while/body/eval_jaxpr/hqk,qhd->khd/dot_general | solution.py:103
  662.1 8.0 fusion.246
  670.1 8.1 fusion.243
  678.2 24.0 %fusion.247 = bf16[4,512,4,64]{1,3,2,0:T(8,128)(2,1)} fusion(bf16[4,512,4,64]{1,3,2,0:T(8,128)(2,1)} %get-tuple-element.537, s32[]{:T(128)S(6)} %copy.184, bf16[2048,4,64]{0,2,1:T(8,128)(2,1)S(1)} %get-tuple-element.554, f32[4,512,2048]{2,1,0:T(8,128)} %fusion.243, f32[4,512,2048]{2,1,0:T(8,128)} %copy-done.2, ...), kind=kOutput, calls=%fused_computation.42.clone.1 | convolution fusion | flops 583012352 | bytes 70795264 | tf_op jit(solution)/shard_map/while/body/eval_jaxpr/hqk,khd->qhd/dot_general | solution.py:100
  702.2 26.1 %fusion.245 = f32[2048,4,64]{0,2,1:T(8,128)} fusion(f32[4,512,2048]{2,1,0:T(8,128)} %fusion.243, f32[4,512,2048]{2,1,0:T(8,128)} %copy-done.2, f32[4,512]{1,0:T(4,128)S(1)} %dynamic-slice_bitcast_fusion.2, pred[512,2048]{1,0:T(8,128)(4,1)S(1)} %broadcast_compare_fusion.5, f32[2048,4,64]{0,2,1:T(8,128)} %get-tuple-element.535, pred[]{:T(512)S(6)} %compare.3, ...), kind=kOutput, calls=%fused_computation.39.clone.1 | convolution fusion | flops 584060928 | bytes 73678856 | tf_op jit(solution)/shard_map/while/body/eval_jaxpr/hqk,qhd->khd/dot_general | solution.py:103
  738.6 4.4 fusion.160
  743.0 4.7 fusion.154
  749.0 7.1 fusion.118
  757.3 6.8 fusion.131
  768.0 4.4 all-to-all-start.3
  776.3 9.2 reduce.38
  788.1 4.2 all-to-all-start.1
  796.2 8.0 reduce.37
  805.8 4.6 all-to-all-done.1
  814.3 5.8 reshape.989
  822.8 5.8 reshape.987
  833.6 7.9 fusion.135
  848.3 8.6 fusion.136
  858.6 103.7 %all-reduce.5.cloned.1.call-done = (bf16[1024,3,256]{2,0,1:T(8,128)(2,1)}, bf16[256,1024]{1,0:T(8,128)(2,1)}, bf16[1024,1024]{1,0:T(8,128)(2,1)}, bf16[1024,1024]{1,0:T(8,128)(2,1)}) async-done(((bf16[1024,3,256]{2,0,1:T(8,128)(2,1)}, bf16[256,1024]{1,0:T(8,128)(2,1)}, bf16[1024,1024]{1,0:T(8,128)(2,1)}, bf16[1024,1024]{1,0:T(8,128)(2,1)}), (bf16[1024,3,256]{2,0,1:T(8,128)(2,1)}, ...) | async-done | bytes 6291472 | tf_op jit(solution)/shard_map/psum | solution.py:334
  973.4 35.0 %reduce-scatter.11.cloned.1.call-done = bf16[512,1,1024]{2,0,1:T(8,128)(2,1)} async-done(((bf16[2048,1,1024]{2,0,1:T(8,128)(2,1)}), bf16[512,1,1024]{2,0,1:T(8,128)(2,1)}) %reduce-scatter.11.cloned.1.call-update) | async-done | bytes 1048592 | tf_op jit(solution)/shard_map/reduce_scatter | solution.py:309
  1014.0 37.5 %all-reduce.1 = (bf16[1024]{0:T(1024)(128)(2,1)S(1)}, bf16[1024]{0:T(1024)(128)(2,1)S(1)}, bf16[1024]{0:T(1024)(128)(2,1)S(1)}, bf16[1024]{0:T(1024)(128)(2,1)S(...) all-reduce(bf16[1024]{0:T(1024)(128)(2,1)S(1)} %copy-done.48, ...), channel_id=1, replica_groups=mesh['section'=2,'rows'=4,'heads'=4] {'section','rows'}, use_global_device_ids=true, to_apply=%region_30.31 | all-reduce | flops 7680 | bytes 30720 | tf_op jit(solution)/shard_map/psum | solution.py:337
  1059.4 10.9 %all-reduce = (f32[1024]{0:T(1024)}, f32[1024]{0:T(1024)}, f32[1024]{0:T(1024)}, f32[1024]{0:T(1024)}, f32[1024]{0:T(1024)}, /*index=5*/f32[1024]{0:T(1024)}) all-reduce(bf16[1024]{0:T(1024)(128)(2,1)S(1)} %get-tuple-element.338, ...), channel_id=1, replica_groups=mesh['section'=2,'rows'=4,'heads'=4] {'heads'}, use_global_device_ids=true, to_apply=%region_31.32 | all-reduce | flops 6144 | bytes 36864 | tf_op jit(solution)/shard_map/psum | solution.py:348
  (313 shorter events, 172.1 us)
Async XLA Ops:
  7.2 238.6 %copy-start = (bf16[1024,1024]{1,0:T(8,128)(2,1)S(1)}, bf16[1024,1024]{1,0:T(8,128)(2,1)}, u32[]{:S(2)}) copy-start(bf16[1024,1024]{1,0:T(8,128)(2,1)} %param.28) | copy-start | bytes 6291460
  7.2 8.0 copy-start.51
  7.2 8.2 copy-start.44
  7.2 45.3 %all-gather.5.cloned.1.call-start = ((), (), s32[]{:S(2)}) async-start(), calls=%async_computation.8 | async-start | bytes 5242880 | tf_op jit(solution)/shard_map/all_gather | solution.py:161
  8.8 7.4 copy-start.31
  11.8 4.5 copy-start.27
  15.1 169.1 %reduce-scatter.5.cloned.1.call-start = ((), (), s32[]{:S(2)}) async-start(), calls=%async_computation.9 | async-start | bytes 5242880 | tf_op jit(solution)/shard_map/reduce_scatter | solution.py:188
  16.1 36.4 %copy-start.34 = (s32[2,6]{0,1:T(8,128)}, s32[2,6]{0,1:T(8,128)S(1)}, u32[]{:S(2)}) copy-start(s32[2,6]{0,1:T(8,128)S(1)} %reduce_window_sum.11) | copy-start | bytes 148
  16.3 36.2 %copy-start.29 = (s32[2,2048]{1,0:T(2,128)}, s32[2,2048]{1,0:T(2,128)S(1)}, u32[]{:S(2)}) copy-start(s32[2,2048]{1,0:T(2,128)S(1)} %fusion.165) | copy-start | bytes 49156
  75.1 4.4 copy-start.8
  75.1 4.4 copy-start.17
  90.8 4.4 copy-start.8
  90.8 4.4 copy-start.17
  106.5 4.4 copy-start.8
  106.5 4.4 copy-start.17
  122.2 4.4 copy-start.8
  139.5 106.2 %all-gather.7.cloned.1.call-start = ((), (), s32[]{:S(2)}) async-start(), calls=%async_computation.10 | async-start | bytes 5242880 | tf_op jit(solution)/shard_map/all_gather | solution.py:200
  139.7 50.4 %copy-start.50 = (s32[2,1,6]{2,1,0:T(1,128)S(1)}, s32[2,1,6]{2,1,0:T(1,128)}, u32[]{:S(2)}) copy-start(s32[2,1,6]{2,1,0:T(1,128)} %param.23) | copy-start | bytes 148
  139.7 50.5 %copy-start.45 = (s32[2,1,6]{2,1,0:T(1,128)S(1)}, s32[2,1,6]{2,1,0:T(1,128)}, u32[]{:S(2)}) copy-start(s32[2,1,6]{2,1,0:T(1,128)} %param.22) | copy-start | bytes 148
  139.7 50.9 %copy-start.35 = (s32[2,6]{0,1:T(8,128)S(1)}, s32[2,6]{0,1:T(8,128)}, u32[]{:S(2)}) copy-start(s32[2,6]{0,1:T(8,128)} %copy-done.34) | copy-start | bytes 148
  139.7 50.9 %copy-start.37 = (s32[2,6]{0,1:T(8,128)S(1)}, s32[2,6]{0,1:T(8,128)}, u32[]{:S(2)}) copy-start(s32[2,6]{0,1:T(8,128)} %copy-done.36) | copy-start | bytes 148
  139.7 50.9 %copy-start.30 = (s32[2,2048]{1,0:T(2,128)S(1)}, s32[2,2048]{1,0:T(2,128)}, u32[]{:S(2)}) copy-start(s32[2,2048]{1,0:T(2,128)} %copy-done.29) | copy-start | bytes 49156
  191.5 7.9 copy-start.42
  205.4 30.0 %all-to-all-start.2 = ((bf16[8,2,32768]{2,1,0:T(2,128)(2,1)}), bf16[8,2,32768]{2,1,0:T(2,128)(2,1)}, u32[]{:S(2)}, u32[]{:S(2)}) async-start(bf16[8,2,32768]{2,1,0:T(2,128)(2,1)} %reshape.982), calls=%async_computation.4 | async-start | bytes 2097152 | tf_op jit(solution)/shard_map/all_to_all | solution.py:229
  209.6 69.8 %all-gather.9.cloned.1.call-start = ((), (), s32[]{:S(2)}) async-start(), calls=%async_computation.12 | async-start | bytes 5242880 | tf_op jit(solution)/shard_map/all_gather | solution.py:247
  212.9 32.9 %copy-start.55 = (bf16[1024]{0:T(1024)(128)(2,1)S(1)}, bf16[1024]{0:T(1024)(128)(2,1)}, u32[]{:S(2)}) copy-start(bf16[1024]{0:T(1024)(128)(2,1)} %param.29) | copy-start | bytes 6148
  245.7 100.4 %reduce-scatter.9.cloned.1.call-start = ((), (), s32[]{:S(2)}) async-start(), calls=%async_computation.13 | async-start | bytes 5242880 | tf_op jit(solution)/shard_map/reduce_scatter | solution.py:259
  301.4 91.6 %reduce-scatter.7.cloned.1.call-start = ((), (), s32[]{:S(2)}) async-start(), calls=%async_computation.11 | async-start | bytes 5242880 | tf_op jit(solution)/shard_map/reduce_scatter | solution.py:207
  311.7 34.3 %copy-start.4 = (bf16[1,512,1,1024]{3,1,2,0:T(8,128)(2,1)S(1)}, bf16[1,512,1,1024]{3,1,2,0:T(8,128)(2,1)}, u32[]{:S(2)}) copy-start(bf16[1,512,1,1024]{3,1,2,0:T(8,128)(2,1)} %param.21) | copy-start | bytes 3145732
  311.7 34.3 %copy-start.7 = (bf16[512,1,1024]{2,0,1:T(8,128)(2,1)S(1)}, bf16[512,1,1024]{2,0,1:T(8,128)(2,1)}, u32[]{:S(2)}) copy-start(bf16[512,1,1024]{2,0,1:T(8,128)(2,1)} %reduce-scatter.5.cloned.1.call-done) | copy-start | bytes 3145732
  311.8 123.7 %all-gather.11.cloned.1.call-start = ((), (), s32[]{:S(2)}) async-start(), calls=%async_computation.14 | async-start | bytes 5242880 | tf_op jit(solution)/shard_map/all_gather | solution.py:272
  393.0 4.6 copy-start.12
  393.0 4.6 copy-start.13
  400.8 561.5 %all-reduce.5.cloned.1.call-start = ((), (), s32[]{:S(2)}) async-start(), calls=%async_computation.16 | async-start | bytes 12582912 | tf_op jit(solution)/shard_map/psum | solution.py:334
  400.9 9.5 copy-start.59
  400.9 9.5 copy-start.65
  410.4 25.1 %copy-start.63 = (bf16[256,1024]{1,0:T(8,128)(2,1)S(1)}, bf16[256,1024]{1,0:T(8,128)(2,1)}, u32[]{:S(2)}) copy-start(bf16[256,1024]{1,0:T(8,128)(2,1)} %param.26) | copy-start | bytes 1572868
  439.0 7.0 copy-start.9
  450.9 6.8 copy-start.2
  520.1 8.1 copy-start.2
  591.1 8.1 copy-start.2
  662.1 8.1 copy-start.2
  738.6 4.4 copy-start.21
  738.6 4.4 copy-start.24
  738.6 4.4 copy-start.26
  738.6 4.4 copy-start.58
  747.8 260.6 %reduce-scatter.11.cloned.1.call-start = ((), (), s32[]{:S(2)}) async-start(), calls=%async_computation.15 | async-start | bytes 5242880 | tf_op jit(solution)/shard_map/reduce_scatter | solution.py:309
  764.1 8.3 copy-start.5
  768.0 20.1 %all-to-all-start.3 = ((bf16[8,2,32768]{2,1,0:T(2,128)(2,1)}), bf16[8,2,32768]{2,1,0:T(2,128)(2,1)}, u32[]{:S(2)}, u32[]{:S(2)}) async-start(bf16[8,2,32768]{2,1,0:T(2,128)(2,1)} %reshape.988), calls=%async_computation.7 | async-start | bytes 2097152 | tf_op jit(solution)/shard_map/all_to_all | solution.py:236
  776.3 16.0 %copy-start.16 = (bf16[512,1,1024]{2,0,1:T(8,128)(2,1)S(1)}, bf16[512,1,1024]{2,0,1:T(8,128)(2,1)}, u32[]{:S(2)}) copy-start(bf16[512,1,1024]{2,0,1:T(8,128)(2,1)} %get-tuple-element.365) | copy-start | bytes 3145732
  788.1 22.4 %all-to-all-start.1 = ((bf16[8,2,32768]{2,1,0:T(2,128)(2,1)}), bf16[8,2,32768]{2,1,0:T(2,128)(2,1)}, u32[]{:S(2)}, u32[]{:S(2)}) async-start(bf16[8,2,32768]{2,1,0:T(2,128)(2,1)} %reshape.986), calls=%async_computation.3 | async-start | bytes 2097152 | tf_op jit(solution)/shard_map/all_to_all | solution.py:220
  796.2 18.0 %copy-start.33 = (s32[2,2048]{1,0:T(2,128)S(1)}, s32[2,2048]{1,0:T(2,128)}, u32[]{:S(2)}) copy-start(s32[2,2048]{1,0:T(2,128)} %get-tuple-element.373) | copy-start | bytes 49156
  810.5 31.1 %all-to-all-start = ((bf16[8,2,32768]{2,1,0:T(2,128)(2,1)}), bf16[8,2,32768]{2,1,0:T(2,128)(2,1)S(1)}, u32[]{:S(2)}, u32[]{:S(2)}) async-start(bf16[8,2,32768]{2,1,0:T(2,128)(2,1)} %reshape.984), calls=%async_computation.2 | async-start | bytes 2097152 | tf_op jit(solution)/shard_map/all_to_all | solution.py:219
  962.3 5.6 copy-start.20
  970.4 37.9 %copy-start.28 = (f32[1024]{0:T(1024)S(1)}, f32[1024]{0:T(1024)}, u32[]{:S(2)}) copy-start(f32[1024]{0:T(1024)} %copy-done.27) | copy-start | bytes 12292
  970.4 37.9 %copy-start.32 = (f32[512]{0:T(512)S(1)}, f32[512]{0:T(512)}, u32[]{:S(2)}) copy-start(f32[512]{0:T(512)} %copy-done.31) | copy-start | bytes 6148
  970.4 39.7 %copy-start.41 = (f32[512]{0:T(512)S(1)}, f32[512]{0:T(512)}, u32[]{:S(2)}) copy-start(f32[512]{0:T(512)} %copy-done.40) | copy-start | bytes 6148
  970.5 41.1 %copy-start.39 = (f32[512]{0:T(512)S(1)}, f32[512]{0:T(512)}, u32[]{:S(2)}) copy-start(f32[512]{0:T(512)} %copy-done.38) | copy-start | bytes 6148
  973.4 40.6 %copy-start.46 = (bf16[1024]{0:T(1024)(128)(2,1)S(1)}, bf16[1024]{0:T(1024)(128)(2,1)}, u32[]{:S(2)}) copy-start(bf16[1024]{0:T(1024)(128)(2,1)} %get-tuple-element.288) | copy-start | bytes 6148
  973.4 40.6 %copy-start.47 = (bf16[1024]{0:T(1024)(128)(2,1)S(1)}, bf16[1024]{0:T(1024)(128)(2,1)}, u32[]{:S(2)}) copy-start(bf16[1024]{0:T(1024)(128)(2,1)} %get-tuple-element.352) | copy-start | bytes 6148
  973.4 40.6 %copy-start.48 = (bf16[1024]{0:T(1024)(128)(2,1)S(1)}, bf16[1024]{0:T(1024)(128)(2,1)}, u32[]{:S(2)}) copy-start(bf16[1024]{0:T(1024)(128)(2,1)} %get-tuple-element.354) | copy-start | bytes 6148
  973.4 40.6 %copy-start.49 = (bf16[1024]{0:T(1024)(128)(2,1)S(1)}, bf16[1024]{0:T(1024)(128)(2,1)}, u32[]{:S(2)}) copy-start(bf16[1024]{0:T(1024)(128)(2,1)} %get-tuple-element.366) | copy-start | bytes 6148
  973.4 40.6 %copy-start.57 = (bf16[1024]{0:T(1024)(128)(2,1)S(1)}, bf16[1024]{0:T(1024)(128)(2,1)}, u32[]{:S(2)}) copy-start(bf16[1024]{0:T(1024)(128)(2,1)} %get-tuple-element.370) | copy-start | bytes 6148
  1052.1 18.2 %copy-start.1 = (bf16[1024,1024]{1,0:T(8,128)(2,1)S(1)}, bf16[1024,1024]{1,0:T(8,128)(2,1)}, u32[]{:S(2)}) copy-start(bf16[1024,1024]{1,0:T(8,128)(2,1)} %param.28) | copy-start | bytes 6291460
  (30 other events, 70.8 us)
Sparse Core Ops, SparseCore 0:
  15.3 37.1 all-gather.4
  139.7 44.4 reduce-scatter.4
  190.2 44.9 all-gather.6
  245.8 33.5 all-gather.8
  301.5 44.4 reduce-scatter.8
  348.4 44.4 reduce-scatter.6
  401.0 34.4 all-gather.10
  747.9 214.4 all-reduce.4
  964.9 43.4 reduce-scatter.10
where the time goes:
time: 1090 us; the launch traced here: 1080 us
  matrix products  445 us (41%)
  waiting for transfers between devices  351 us (32%)
  other arithmetic  104 us (10%)
  local copies, waits for them, and re-layouts  95.7 us (9%)
  blocking collectives  48.4 us (4%)
  starting transfers between devices  17.1 us (2%)
  between operations  15 us (1%)
    psum x1, waiting for transfers between devices, per_device(): lax.psum(grad_w_qkv_part.astype(jnp.bfloat16), ('section', 'rows'))  104 us
    dot_general x4, matrix products, one_block(): jnp.einsum('hqk,qhd->khd', grad_score, queries, preferred_element_type=jn...  104 us
    dot_general x4, matrix products, one_block(): jnp.einsum('hqk,khd->qhd', grad_score, key_seq, preferred_element_type=jn...  96 us
    unnamed x136, local copies, waits for them, and re-layouts  51.9 us
    reduce_scatter x1, waiting for transfers between devices, per_device(): lax.psum_scatter(jnp.einsum('rsf,fd->rsd', picked, w_down, preferred_elem...  45 us
    reduce_scatter x1, waiting for transfers between devices, per_device(): lax.psum_scatter(jnp.einsum('rsk,kd->rsd', picked, w_out, preferred_eleme...  44.5 us
    psum x1, blocking collectives, per_device(): lax.psum(grad_b_out.astype(jnp.bfloat16), ('section', 'rows'))  37.5 us
    all_gather x1, waiting for transfers between devices, per_device(): gathered_one = lax.all_gather(normed_one, 'heads', axis=0, tiled=True)  35 us
  transfers between devices with their start and end apart: 13, of which 10 were waited for; matrix products, arithmetic and copies ran while one was open for 17% of the time, Pallas kernels for 0%

commit v1 on v0

--- a/solution.py
+++ b/solution.py
@@ -334,7 +334,9 @@
         lax.psum(grad_w_qkv_part.astype(jnp.bfloat16), ("section", "rows")).astype(jnp.float32),
         lax.psum(grad_b_qv.astype(jnp.bfloat16), ("section", "rows")).astype(jnp.float32),
         lax.psum(grad_w_out_part.astype(jnp.bfloat16), ("section", "rows")).astype(jnp.float32),
-        lax.psum(grad_b_out.astype(jnp.bfloat16), ("section", "rows")).astype(jnp.float32),
+        jnp.sum(
+            lax.all_gather(grad_b_out.astype(jnp.bfloat16), ("section", "rows")), axis=0
+        ).astype(jnp.float32),
         lax.psum(grad_gain_one, ("section", "rows")).astype(jnp.float32),
         lax.psum(grad_shift_one, ("section", "rows")).astype(jnp.float32),
         lax.psum(grad_w_up_part.astype(jnp.bfloat16), ("section", "rows")).astype(jnp.float32),

time: 1090 us -> 1090 us (level)
  blocking collectives: 48.4 us -> 75.8 us
  waiting for transfers between devices: 351 us -> 324 us
    all_gather x0 -> x1, blocking collectives: none -> 27.6 us  [per_device(): lax.all_gather(grad_b_out.astype(jnp.bfloat16), ('section', 'rows'))]
    psum x1, waiting for transfers between devices: 104 us -> 76.6 us  [per_device(): lax.psum(grad_w_qkv_part.astype(jnp.bfloat16), ('section', 'rows'))]
where the time goes in v1:
time: 1090 us; the launch traced here: 1080 us
  matrix products  445 us (41%)
  waiting for transfers between devices  324 us (30%)
  other arithmetic  104 us (10%)
  local copies, waits for them, and re-layouts  95.8 us (9%)
  blocking collectives  75.8 us (7%)
  starting transfers between devices  16.8 us (2%)
  between operations  14.8 us (1%)
    dot_general x4, matrix products, one_block(): jnp.einsum('hqk,qhd->khd', grad_score, queries, preferred_element_type=jn...  104 us
    dot_general x4, matrix products, one_block(): jnp.einsum('hqk,khd->qhd', grad_score, key_seq, preferred_element_type=jn...  96 us
    psum x1, waiting for transfers between devices, per_device(): lax.psum(grad_w_qkv_part.astype(jnp.bfloat16), ('section', 'rows'))  76.6 us
    unnamed x136, local copies, waits for them, and re-layouts  52.1 us
    reduce_scatter x1, waiting for transfers between devices, per_device(): lax.psum_scatter(jnp.einsum('rsf,fd->rsd', picked, w_down, preferred_elem...  44.9 us
    reduce_scatter x1, waiting for transfers between devices, per_device(): lax.psum_scatter(jnp.einsum('rsk,kd->rsd', picked, w_out, preferred_eleme...  44.5 us
    psum x1, blocking collectives, per_device(): lax.psum(grad_b_down.astype(jnp.bfloat16), ('section', 'rows'))  37.3 us
    all_gather x1, waiting for transfers between devices, per_device(): gathered_one = lax.all_gather(normed_one, 'heads', axis=0, tiled=True)  35 us
  transfers between devices with their start and end apart: 13, of which 10 were waited for; matrix products, arithmetic and copies ran while one was open for 17% of the time, Pallas kernels for 0%

profile of v1, /device:TPU:0, one launch (start us, length us, event | category | flops | bytes accessed | tf_op | source)
XLA Modules:
  0.0 1077.4 jit_solution(12064455370518345605)
XLA Ops:
  17.5 35.0 %all-gather.6.cloned.1.call-done = bf16[2048,1,1024]{2,0,1:T(8,128)(2,1)} async-done(((bf16[512,1,1024]{2,0,1:T(8,128)(2,1)}), bf16[2048,1,1024]{2,0,1:T(8,128)(2,1)}) %all-gather.6.cloned.1.call-update) | async-done | bytes 4194320 | tf_op jit(solution)/shard_map/all_gather | solution.py:161
  52.5 5.8 fusion.115
  69.9 63.2 %while.27 = (s32[]{:T(128)}, bf16[4,512,4,64]{1,3,2,0:T(8,128)(2,1)}, f32[4,4,512]{2,1,0:T(4,128)}, s32[4,512]{1,0:T(4,128)S(1)}, s32[1,2048]{1,0:T(1,128)S(1)},...) while((s32[]{:T(128)}, ...), condition=%wide.region_7.8_spmd, body=%wide.region_4.7_spmd.sunk | while | flops 1125120000 | bytes 70072528 | solution.py:78
  70.6 4.5 fusion.230
  75.1 4.4 fusion.231
  79.6 5.1 fusion.232
  86.3 4.5 fusion.230
  90.8 4.4 fusion.231
  95.3 5.1 fusion.232
  102.0 4.5 fusion.230
  106.5 4.4 fusion.231
  110.9 5.1 fusion.232
  117.7 4.5 fusion.230
  122.2 4.4 fusion.231
  126.6 5.1 fusion.232
  140.0 44.5 %reduce-scatter.5.cloned.1.call-done = bf16[512,1,1024]{2,0,1:T(8,128)(2,1)} async-done(((bf16[2048,1,1024]{2,0,1:T(8,128)(2,1)}), bf16[512,1,1024]{2,0,1:T(8,128)(2,1)}) %reduce-scatter.5.cloned.1.call-update) | async-done | bytes 1048592 | tf_op jit(solution)/shard_map/reduce_scatter | solution.py:188
  191.8 7.9 fusion.130
  213.0 22.6 %all-to-all-done.2 = bf16[8,2,32768]{2,1,0:T(2,128)(2,1)} async-done(((bf16[8,2,32768]{2,1,0:T(2,128)(2,1)}), bf16[8,2,32768]{2,1,0:T(2,128)(2,1)}, u32[]{:S(2)}, u32[]{:S(2)}) %all-to-all-start.2) | async-done | bytes 1048608 | tf_op jit(solution)/shard_map/all_to_all | solution.py:229
  235.6 5.8 reshape.984
  246.1 25.8 %multiply_convert_fusion.1 = (bf16[2048,1024]{1,0:T(8,128)(2,1)}, f32[2048,1024]{1,0:T(8,128)}, f32[2048,1024]{1,0:T(8,128)}) fusion(f32[1024]{0:T(1024)S(1)} %convert_element_type.443, bf16[1024,1024]{1,0:T(8,128)(2,1)S(1)} %copy-done, bf16[2048,1,1024]{2,0,1:T(8,128)(2,1)} %all-gather.8.cloned.1.call-done), kind=kOutput, calls=%fused_computation.81 | convolution fusion | flops 4433379328 | bytes 27267072 | tf_op jit(solution)/shard_map/rsd,df->rsf/dot_general | solution.py:202
  271.9 7.8 all-gather.10.cloned.1.call-done
  279.7 13.9 %fusion.186 = (bf16[1024]{0:T(1024)(128)(2,1)}, bf16[2048,1024]{1,0:T(8,128)(2,1)S(1)}) fusion(f32[2048,1024]{1,0:T(8,128)} %get-tuple-element.357, bf16[1024,1024]{1,0:T(8,128)(2,1)} %param.30, bf16[2048,1,1024]{2,0,1:T(8,128)(2,1)} %all-gather.10.cloned.1.call-done, f32[2048,1024]{1,0:T(8,128)} %get-tuple-element.368, f32[1024]{0:T(1024)S(1)} %convert_element_type.443), kind=kOutput, calls=%fused_computation.215 | convolution fusion | flops 4328520704 | bytes 27269120 | tf_op jit(solution)/shard_map/rsd,fd->rsf/dot_general | solution.py:251
  295.6 6.1 convert_bitcast_fusion
  303.2 8.7 convert_bitcast_fusion.1
  312.6 33.7 %reduce-scatter.9.cloned.1.call-done = bf16[512,1,1024]{2,0,1:T(8,128)(2,1)} async-done(((bf16[2048,1,1024]{2,0,1:T(8,128)(2,1)}), bf16[512,1,1024]{2,0,1:T(8,128)(2,1)}) %reduce-scatter.9.cloned.1.call-update) | async-done | bytes 1048592 | tf_op jit(solution)/shard_map/reduce_scatter | solution.py:259
  348.3 44.9 %reduce-scatter.7.cloned.1.call-done = bf16[512,1,1024]{2,0,1:T(8,128)(2,1)} async-done(((bf16[2048,1,1024]{2,0,1:T(8,128)(2,1)}), bf16[512,1,1024]{2,0,1:T(8,128)(2,1)}) %reduce-scatter.7.cloned.1.call-update) | async-done | bytes 1048592 | tf_op jit(solution)/shard_map/reduce_scatter | solution.py:207
  393.3 4.6 fusion.141
  401.2 9.5 fusion.150
  410.7 5.8 fusion.147
  416.5 19.3 %all-gather.12.cloned.1.call-done = bf16[2048,1,1024]{2,0,1:T(8,128)(2,1)} async-done(((bf16[512,1,1024]{2,0,1:T(8,128)(2,1)}), bf16[2048,1,1024]{2,0,1:T(8,128)(2,1)}) %all-gather.12.cloned.1.call-update) | async-done | bytes 4194320 | tf_op jit(solution)/shard_map/all_gather | solution.py:272
  446.2 282.8 %while.28 = (s32[]{:T(128)}, f32[2048,4,64]{0,2,1:T(8,128)}, f32[2048,4,64]{0,2,1:T(8,128)}, bf16[4,512,4,64]{1,3,2,0:T(8,128)(2,1)}, bf16[4,512,4,64]{1,3,2,0:T...) while((s32[]{:T(128)}, f32[2048,4,64]{0,2,1:T(8,128)}, ...), condition=%wide.region_20.21_spmd.clone, body=%wide.region_18.20_spmd.clone.sunk | while | flops 2796560384 | bytes 275323104 | solution.py:112
  451.2 6.8 fusion.246
  458.0 8.1 fusion.243
  466.1 24.0 %fusion.247 = bf16[4,512,4,64]{1,3,2,0:T(8,128)(2,1)} fusion(bf16[4,512,4,64]{1,3,2,0:T(8,128)(2,1)} %get-tuple-element.536, s32[]{:T(128)S(6)} %copy.184, bf16[2048,4,64]{0,2,1:T(8,128)(2,1)S(1)} %get-tuple-element.553, f32[4,512,2048]{2,1,0:T(8,128)} %fusion.243, f32[4,512,2048]{2,1,0:T(8,128)} %copy-done.2, ...), kind=kOutput, calls=%fused_computation.42.clone.1 | convolution fusion | flops 583012352 | bytes 70795264 | tf_op jit(solution)/shard_map/while/body/eval_jaxpr/hqk,khd->qhd/dot_general | solution.py:100
  490.1 25.5 %fusion.245 = f32[2048,4,64]{0,2,1:T(8,128)} fusion(f32[4,512,2048]{2,1,0:T(8,128)} %fusion.243, f32[4,512,2048]{2,1,0:T(8,128)} %copy-done.2, f32[4,512]{1,0:T(4,128)S(1)} %dynamic-slice_bitcast_fusion.2, pred[512,2048]{1,0:T(8,128)(4,1)S(1)} %broadcast_compare_fusion.5, f32[2048,4,64]{0,2,1:T(8,128)} %get-tuple-element.534, pred[]{:T(512)S(6)} %compare.3, ...), kind=kOutput, calls=%fused_computation.39.clone.1 | convolution fusion | flops 584060928 | bytes 73678856 | tf_op jit(solution)/shard_map/while/body/eval_jaxpr/hqk,qhd->khd/dot_general | solution.py:103
  520.4 8.0 fusion.246
  528.4 8.1 fusion.243
  536.5 24.0 %fusion.247 = bf16[4,512,4,64]{1,3,2,0:T(8,128)(2,1)} fusion(bf16[4,512,4,64]{1,3,2,0:T(8,128)(2,1)} %get-tuple-element.536, s32[]{:T(128)S(6)} %copy.184, bf16[2048,4,64]{0,2,1:T(8,128)(2,1)S(1)} %get-tuple-element.553, f32[4,512,2048]{2,1,0:T(8,128)} %fusion.243, f32[4,512,2048]{2,1,0:T(8,128)} %copy-done.2, ...), kind=kOutput, calls=%fused_computation.42.clone.1 | convolution fusion | flops 583012352 | bytes 70795264 | tf_op jit(solution)/shard_map/while/body/eval_jaxpr/hqk,khd->qhd/dot_general | solution.py:100
  560.5 26.1 %fusion.245 = f32[2048,4,64]{0,2,1:T(8,128)} fusion(f32[4,512,2048]{2,1,0:T(8,128)} %fusion.243, f32[4,512,2048]{2,1,0:T(8,128)} %copy-done.2, f32[4,512]{1,0:T(4,128)S(1)} %dynamic-slice_bitcast_fusion.2, pred[512,2048]{1,0:T(8,128)(4,1)S(1)} %broadcast_compare_fusion.5, f32[2048,4,64]{0,2,1:T(8,128)} %get-tuple-element.534, pred[]{:T(512)S(6)} %compare.3, ...), kind=kOutput, calls=%fused_computation.39.clone.1 | convolution fusion | flops 584060928 | bytes 73678856 | tf_op jit(solution)/shard_map/while/body/eval_jaxpr/hqk,qhd->khd/dot_general | solution.py:103
  591.4 8.0 fusion.246
  599.5 8.1 fusion.243
  607.6 24.0 %fusion.247 = bf16[4,512,4,64]{1,3,2,0:T(8,128)(2,1)} fusion(bf16[4,512,4,64]{1,3,2,0:T(8,128)(2,1)} %get-tuple-element.536, s32[]{:T(128)S(6)} %copy.184, bf16[2048,4,64]{0,2,1:T(8,128)(2,1)S(1)} %get-tuple-element.553, f32[4,512,2048]{2,1,0:T(8,128)} %fusion.243, f32[4,512,2048]{2,1,0:T(8,128)} %copy-done.2, ...), kind=kOutput, calls=%fused_computation.42.clone.1 | convolution fusion | flops 583012352 | bytes 70795264 | tf_op jit(solution)/shard_map/while/body/eval_jaxpr/hqk,khd->qhd/dot_general | solution.py:100
  631.6 26.1 %fusion.245 = f32[2048,4,64]{0,2,1:T(8,128)} fusion(f32[4,512,2048]{2,1,0:T(8,128)} %fusion.243, f32[4,512,2048]{2,1,0:T(8,128)} %copy-done.2, f32[4,512]{1,0:T(4,128)S(1)} %dynamic-slice_bitcast_fusion.2, pred[512,2048]{1,0:T(8,128)(4,1)S(1)} %broadcast_compare_fusion.5, f32[2048,4,64]{0,2,1:T(8,128)} %get-tuple-element.534, pred[]{:T(512)S(6)} %compare.3, ...), kind=kOutput, calls=%fused_computation.39.clone.1 | convolution fusion | flops 584060928 | bytes 73678856 | tf_op jit(solution)/shard_map/while/body/eval_jaxpr/hqk,qhd->khd/dot_general | solution.py:103
  662.4 8.0 fusion.246
  670.5 8.1 fusion.243
  678.6 24.0 %fusion.247 = bf16[4,512,4,64]{1,3,2,0:T(8,128)(2,1)} fusion(bf16[4,512,4,64]{1,3,2,0:T(8,128)(2,1)} %get-tuple-element.536, s32[]{:T(128)S(6)} %copy.184, bf16[2048,4,64]{0,2,1:T(8,128)(2,1)S(1)} %get-tuple-element.553, f32[4,512,2048]{2,1,0:T(8,128)} %fusion.243, f32[4,512,2048]{2,1,0:T(8,128)} %copy-done.2, ...), kind=kOutput, calls=%fused_computation.42.clone.1 | convolution fusion | flops 583012352 | bytes 70795264 | tf_op jit(solution)/shard_map/while/body/eval_jaxpr/hqk,khd->qhd/dot_general | solution.py:100
  702.6 26.1 %fusion.245 = f32[2048,4,64]{0,2,1:T(8,128)} fusion(f32[4,512,2048]{2,1,0:T(8,128)} %fusion.243, f32[4,512,2048]{2,1,0:T(8,128)} %copy-done.2, f32[4,512]{1,0:T(4,128)S(1)} %dynamic-slice_bitcast_fusion.2, pred[512,2048]{1,0:T(8,128)(4,1)S(1)} %broadcast_compare_fusion.5, f32[2048,4,64]{0,2,1:T(8,128)} %get-tuple-element.534, pred[]{:T(512)S(6)} %compare.3, ...), kind=kOutput, calls=%fused_computation.39.clone.1 | convolution fusion | flops 584060928 | bytes 73678856 | tf_op jit(solution)/shard_map/while/body/eval_jaxpr/hqk,qhd->khd/dot_general | solution.py:103
  738.9 4.4 fusion.160
  743.4 4.7 fusion.154
  749.3 7.1 fusion.118
  757.7 6.7 fusion.131
  776.4 9.1 reduce.39
  788.0 4.4 all-to-all-start.1
  796.4 8.0 reduce.38
  805.9 4.7 all-to-all-done.1
  814.2 5.8 reshape.990
  822.7 5.8 reshape.988
  833.6 7.9 fusion.135
  841.5 27.6 %all-gather = bf16[8192]{0:T(1024)(128)(2,1)S(1)} all-gather(bf16[1024]{0:T(1024)(128)(2,1)S(1)} %copy-done.48), channel_id=2, replica_groups=mesh['section'=2,'rows'=4,'heads'=4] {'section','rows'}, dimensions={0}, use_global_device_ids=true | all-gather | bytes 18432 | tf_op jit(solution)/shard_map/all_gather | solution.py:338
  876.0 8.6 fusion.136
  886.4 76.6 %all-reduce.5.cloned.1.call-done = (bf16[1024,3,256]{2,0,1:T(8,128)(2,1)}, bf16[256,1024]{1,0:T(8,128)(2,1)}, bf16[1024,1024]{1,0:T(8,128)(2,1)}, bf16[1024,1024]{1,0:T(8,128)(2,1)}) async-done(((bf16[1024,3,256]{2,0,1:T(8,128)(2,1)}, bf16[256,1024]{1,0:T(8,128)(2,1)}, bf16[1024,1024]{1,0:T(8,128)(2,1)}, bf16[1024,1024]{1,0:T(8,128)(2,1)}), (bf16[1024,3,256]{2,0,1:T(8,128)(2,1)}, ...) | async-done | bytes 6291472 | tf_op jit(solution)/shard_map/psum | solution.py:334
  974.0 35.0 %reduce-scatter.11.cloned.1.call-done = bf16[512,1,1024]{2,0,1:T(8,128)(2,1)} async-done(((bf16[2048,1,1024]{2,0,1:T(8,128)(2,1)}), bf16[512,1,1024]{2,0,1:T(8,128)(2,1)}) %reduce-scatter.11.cloned.1.call-update) | async-done | bytes 1048592 | tf_op jit(solution)/shard_map/reduce_scatter | solution.py:309
  1014.6 37.3 %all-reduce.1 = (bf16[1024]{0:T(1024)(128)(2,1)S(1)}, bf16[1024]{0:T(1024)(128)(2,1)S(1)}, bf16[1024]{0:T(1024)(128)(2,1)S(1)}, bf16[1024]{0:T(1024)(128)(2,1)S(...) all-reduce(bf16[1024]{0:T(1024)(128)(2,1)S(1)} %copy-done.47, ...), channel_id=1, replica_groups=mesh['section'=2,'rows'=4,'heads'=4] {'section','rows'}, use_global_device_ids=true, to_apply=%region_37.38 | all-reduce | flops 6656 | bytes 26624 | tf_op jit(solution)/shard_map/psum | solution.py:345
  1059.7 10.9 %all-reduce = (f32[1024]{0:T(1024)}, f32[1024]{0:T(1024)}, f32[1024]{0:T(1024)}, f32[1024]{0:T(1024)}, f32[1024]{0:T(1024)}, /*index=5*/f32[1024]{0:T(1024)}) all-reduce(bf16[1024]{0:T(1024)(128)(2,1)S(1)} %reduce_sum.300, bf16[1024]{0:T(1024)(128)(2,1)S(1)} %get-tuple-element.338, ...), channel_id=1, replica_groups=mesh['section'=2,'rows'=4,'heads'=4] {'heads'}, use_global_device_ids=true, to_apply=%region_31.32 | all-reduce | flops 6144 | bytes 36864 | tf_op jit(solution)/shard_map/psum | solution.py:350
  (316 shorter events, 176.1 us)
Async XLA Ops:
  7.2 238.9 %copy-start = (bf16[1024,1024]{1,0:T(8,128)(2,1)S(1)}, bf16[1024,1024]{1,0:T(8,128)(2,1)}, u32[]{:S(2)}) copy-start(bf16[1024,1024]{1,0:T(8,128)(2,1)} %param.28) | copy-start | bytes 6291460
  7.2 8.0 copy-start.51
  7.2 8.2 copy-start.44
  7.2 45.2 %all-gather.6.cloned.1.call-start = ((), (), s32[]{:S(2)}) async-start(), calls=%async_computation.8 | async-start | bytes 5242880 | tf_op jit(solution)/shard_map/all_gather | solution.py:161
  8.8 7.4 copy-start.31
  11.8 4.5 copy-start.27
  15.1 169.4 %reduce-scatter.5.cloned.1.call-start = ((), (), s32[]{:S(2)}) async-start(), calls=%async_computation.9 | async-start | bytes 5242880 | tf_op jit(solution)/shard_map/reduce_scatter | solution.py:188
  16.1 36.4 %copy-start.34 = (s32[2,6]{0,1:T(8,128)}, s32[2,6]{0,1:T(8,128)S(1)}, u32[]{:S(2)}) copy-start(s32[2,6]{0,1:T(8,128)S(1)} %reduce_window_sum.11) | copy-start | bytes 148
  16.2 36.2 %copy-start.29 = (s32[2,2048]{1,0:T(2,128)}, s32[2,2048]{1,0:T(2,128)S(1)}, u32[]{:S(2)}) copy-start(s32[2,2048]{1,0:T(2,128)S(1)} %fusion.165) | copy-start | bytes 49156
  75.1 4.4 copy-start.8
  75.1 4.4 copy-start.17
  90.8 4.4 copy-start.8
  90.8 4.4 copy-start.17
  106.5 4.4 copy-start.8
  106.5 4.4 copy-start.17
  122.2 4.4 copy-start.8
  139.8 106.2 %all-gather.8.cloned.1.call-start = ((), (), s32[]{:S(2)}) async-start(), calls=%async_computation.10 | async-start | bytes 5242880 | tf_op jit(solution)/shard_map/all_gather | solution.py:200
  139.9 50.4 %copy-start.50 = (s32[2,1,6]{2,1,0:T(1,128)S(1)}, s32[2,1,6]{2,1,0:T(1,128)}, u32[]{:S(2)}) copy-start(s32[2,1,6]{2,1,0:T(1,128)} %param.23) | copy-start | bytes 148
  140.0 50.5 %copy-start.45 = (s32[2,1,6]{2,1,0:T(1,128)S(1)}, s32[2,1,6]{2,1,0:T(1,128)}, u32[]{:S(2)}) copy-start(s32[2,1,6]{2,1,0:T(1,128)} %param.22) | copy-start | bytes 148
  140.0 50.9 %copy-start.35 = (s32[2,6]{0,1:T(8,128)S(1)}, s32[2,6]{0,1:T(8,128)}, u32[]{:S(2)}) copy-start(s32[2,6]{0,1:T(8,128)} %copy-done.34) | copy-start | bytes 148
  140.0 50.9 %copy-start.37 = (s32[2,6]{0,1:T(8,128)S(1)}, s32[2,6]{0,1:T(8,128)}, u32[]{:S(2)}) copy-start(s32[2,6]{0,1:T(8,128)} %copy-done.36) | copy-start | bytes 148
  140.0 50.9 %copy-start.30 = (s32[2,2048]{1,0:T(2,128)S(1)}, s32[2,2048]{1,0:T(2,128)}, u32[]{:S(2)}) copy-start(s32[2,2048]{1,0:T(2,128)} %copy-done.29) | copy-start | bytes 49156
  191.8 7.9 copy-start.42
  205.5 30.1 %all-to-all-start.2 = ((bf16[8,2,32768]{2,1,0:T(2,128)(2,1)}), bf16[8,2,32768]{2,1,0:T(2,128)(2,1)}, u32[]{:S(2)}, u32[]{:S(2)}) async-start(bf16[8,2,32768]{2,1,0:T(2,128)(2,1)} %reshape.983), calls=%async_computation.4 | async-start | bytes 2097152 | tf_op jit(solution)/shard_map/all_to_all | solution.py:229
  209.8 69.9 %all-gather.10.cloned.1.call-start = ((), (), s32[]{:S(2)}) async-start(), calls=%async_computation.12 | async-start | bytes 5242880 | tf_op jit(solution)/shard_map/all_gather | solution.py:247
  213.0 33.0 %copy-start.55 = (bf16[1024]{0:T(1024)(128)(2,1)S(1)}, bf16[1024]{0:T(1024)(128)(2,1)}, u32[]{:S(2)}) copy-start(bf16[1024]{0:T(1024)(128)(2,1)} %param.29) | copy-start | bytes 6148
  246.0 100.4 %reduce-scatter.9.cloned.1.call-start = ((), (), s32[]{:S(2)}) async-start(), calls=%async_computation.13 | async-start | bytes 5242880 | tf_op jit(solution)/shard_map/reduce_scatter | solution.py:259
  301.7 91.6 %reduce-scatter.7.cloned.1.call-start = ((), (), s32[]{:S(2)}) async-start(), calls=%async_computation.11 | async-start | bytes 5242880 | tf_op jit(solution)/shard_map/reduce_scatter | solution.py:207
  312.0 34.4 %copy-start.4 = (bf16[1,512,1,1024]{3,1,2,0:T(8,128)(2,1)S(1)}, bf16[1,512,1,1024]{3,1,2,0:T(8,128)(2,1)}, u32[]{:S(2)}) copy-start(bf16[1,512,1,1024]{3,1,2,0:T(8,128)(2,1)} %param.21) | copy-start | bytes 3145732
  312.0 34.4 %copy-start.7 = (bf16[512,1,1024]{2,0,1:T(8,128)(2,1)S(1)}, bf16[512,1,1024]{2,0,1:T(8,128)(2,1)}, u32[]{:S(2)}) copy-start(bf16[512,1,1024]{2,0,1:T(8,128)(2,1)} %reduce-scatter.5.cloned.1.call-done) | copy-start | bytes 3145732
  312.0 123.8 %all-gather.12.cloned.1.call-start = ((), (), s32[]{:S(2)}) async-start(), calls=%async_computation.14 | async-start | bytes 5242880 | tf_op jit(solution)/shard_map/all_gather | solution.py:272
  393.2 4.6 copy-start.12
  393.3 4.6 copy-start.13
  401.1 561.8 %all-reduce.5.cloned.1.call-start = ((), (), s32[]{:S(2)}) async-start(), calls=%async_computation.16 | async-start | bytes 12582912 | tf_op jit(solution)/shard_map/psum | solution.py:334
  401.2 9.5 copy-start.59
  401.2 9.5 copy-start.65
  410.7 25.1 %copy-start.63 = (bf16[256,1024]{1,0:T(8,128)(2,1)S(1)}, bf16[256,1024]{1,0:T(8,128)(2,1)}, u32[]{:S(2)}) copy-start(bf16[256,1024]{1,0:T(8,128)(2,1)} %param.26) | copy-start | bytes 1572868
  439.3 6.9 copy-start.9
  451.2 6.8 copy-start.2
  520.4 8.1 copy-start.2
  591.4 8.1 copy-start.2
  662.4 8.1 copy-start.2
  738.9 4.5 copy-start.21
  738.9 4.5 copy-start.24
  738.9 4.5 copy-start.26
  738.9 4.5 copy-start.58
  748.1 260.9 %reduce-scatter.11.cloned.1.call-start = ((), (), s32[]{:S(2)}) async-start(), calls=%async_computation.15 | async-start | bytes 5242880 | tf_op jit(solution)/shard_map/reduce_scatter | solution.py:309
  764.4 8.1 copy-start.5
  768.2 19.8 %all-to-all-start.3 = ((bf16[8,2,32768]{2,1,0:T(2,128)(2,1)}), bf16[8,2,32768]{2,1,0:T(2,128)(2,1)}, u32[]{:S(2)}, u32[]{:S(2)}) async-start(bf16[8,2,32768]{2,1,0:T(2,128)(2,1)} %reshape.989), calls=%async_computation.7 | async-start | bytes 2097152 | tf_op jit(solution)/shard_map/all_to_all | solution.py:236
  776.4 16.1 %copy-start.16 = (bf16[512,1,1024]{2,0,1:T(8,128)(2,1)S(1)}, bf16[512,1,1024]{2,0,1:T(8,128)(2,1)}, u32[]{:S(2)}) copy-start(bf16[512,1,1024]{2,0,1:T(8,128)(2,1)} %get-tuple-element.364) | copy-start | bytes 3145732
  788.0 22.6 %all-to-all-start.1 = ((bf16[8,2,32768]{2,1,0:T(2,128)(2,1)}), bf16[8,2,32768]{2,1,0:T(2,128)(2,1)}, u32[]{:S(2)}, u32[]{:S(2)}) async-start(bf16[8,2,32768]{2,1,0:T(2,128)(2,1)} %reshape.987), calls=%async_computation.3 | async-start | bytes 2097152 | tf_op jit(solution)/shard_map/all_to_all | solution.py:220
  796.4 17.8 %copy-start.33 = (s32[2,2048]{1,0:T(2,128)S(1)}, s32[2,2048]{1,0:T(2,128)}, u32[]{:S(2)}) copy-start(s32[2,2048]{1,0:T(2,128)} %get-tuple-element.372) | copy-start | bytes 49156
  810.6 58.5 %all-to-all-start = ((bf16[8,2,32768]{2,1,0:T(2,128)(2,1)}), bf16[8,2,32768]{2,1,0:T(2,128)(2,1)S(1)}, u32[]{:S(2)}, u32[]{:S(2)}) async-start(bf16[8,2,32768]{2,1,0:T(2,128)(2,1)} %reshape.985), calls=%async_computation.2 | async-start | bytes 2097152 | tf_op jit(solution)/shard_map/all_to_all | solution.py:219
  833.6 7.9 copy-start.48
  963.0 5.6 copy-start.20
  971.1 37.9 %copy-start.28 = (f32[1024]{0:T(1024)S(1)}, f32[1024]{0:T(1024)}, u32[]{:S(2)}) copy-start(f32[1024]{0:T(1024)} %copy-done.27) | copy-start | bytes 12292
  971.1 37.9 %copy-start.32 = (f32[512]{0:T(512)S(1)}, f32[512]{0:T(512)}, u32[]{:S(2)}) copy-start(f32[512]{0:T(512)} %copy-done.31) | copy-start | bytes 6148
  971.1 39.7 %copy-start.41 = (f32[512]{0:T(512)S(1)}, f32[512]{0:T(512)}, u32[]{:S(2)}) copy-start(f32[512]{0:T(512)} %copy-done.40) | copy-start | bytes 6148
  971.1 41.1 %copy-start.39 = (f32[512]{0:T(512)S(1)}, f32[512]{0:T(512)}, u32[]{:S(2)}) copy-start(f32[512]{0:T(512)} %copy-done.38) | copy-start | bytes 6148
  974.0 40.6 %copy-start.46 = (bf16[1024]{0:T(1024)(128)(2,1)S(1)}, bf16[1024]{0:T(1024)(128)(2,1)}, u32[]{:S(2)}) copy-start(bf16[1024]{0:T(1024)(128)(2,1)} %get-tuple-element.288) | copy-start | bytes 6148
  974.0 40.6 %copy-start.47 = (bf16[1024]{0:T(1024)(128)(2,1)S(1)}, bf16[1024]{0:T(1024)(128)(2,1)}, u32[]{:S(2)}) copy-start(bf16[1024]{0:T(1024)(128)(2,1)} %get-tuple-element.354) | copy-start | bytes 6148
  974.0 40.6 %copy-start.49 = (bf16[1024]{0:T(1024)(128)(2,1)S(1)}, bf16[1024]{0:T(1024)(128)(2,1)}, u32[]{:S(2)}) copy-start(bf16[1024]{0:T(1024)(128)(2,1)} %get-tuple-element.365) | copy-start | bytes 6148
  974.0 40.6 %copy-start.57 = (bf16[1024]{0:T(1024)(128)(2,1)S(1)}, bf16[1024]{0:T(1024)(128)(2,1)}, u32[]{:S(2)}) copy-start(bf16[1024]{0:T(1024)(128)(2,1)} %get-tuple-element.369) | copy-start | bytes 6148
  1052.5 18.2 %copy-start.1 = (bf16[1024,1024]{1,0:T(8,128)(2,1)S(1)}, bf16[1024,1024]{1,0:T(8,128)(2,1)}, u32[]{:S(2)}) copy-start(bf16[1024,1024]{1,0:T(8,128)(2,1)} %param.28) | copy-start | bytes 6291460
  (30 other events, 70.8 us)
Sparse Core Ops, SparseCore 0:
  15.3 37.1 all-gather.5
  140.0 44.4 reduce-scatter.4
  190.5 45.0 all-gather.7
  246.1 33.5 all-gather.9
  301.8 44.5 reduce-scatter.8
  348.7 44.4 reduce-scatter.6
  401.3 34.4 all-gather.11
  748.2 214.6 all-reduce.4
  965.5 43.4 reduce-scatter.10
